TPU v7x, 32 devices: a whole 2x2x4 slice. The times are simulated.
32 devices in a mesh: dp: 4 (over x, core), mp: 8 (over z, y).
Axes of the slice: x: 2, y: 2, z: 4, core: 2. Of those that a mesh axis runs over, the one named last changes fastest.
Arguments:
- hidden: bfloat16 [4, 4, 512, 2048], P('dp', None, None, 'mp'), may hold values from -6 to 6
- gain: float32 [2048], P('mp'), may hold values from 0.1 to 1.9
- cotangent: bfloat16 [4, 4, 512, 2048], P('dp', None, None, 'mp'), may hold values from -600 to 600
- blocks: int32 [4, 4, 2], P('dp'), may hold values from 1 to 2
- loss_mask: int32 [4, 4, 512], P('dp'), may hold values 0 or 1
- wi_gate: bfloat16 [5120, 2048], P('mp'), may hold values from -0.125 to 0.125
- wi_up: bfloat16 [5120, 2048], P('mp'), may hold values from -0.125 to 0.125
- wo_weight: bfloat16 [5120, 2048], P('mp'), may hold values from -0.078125 to 0.078125
Outputs:
- gradients: float32 [3, 5120, 2048], P(None, 'mp')
Inputs may be any that keep to these rules, and one draw needn't show every extreme that they name: blocks of 128 target positions used by a sequence; later positions are padding.
All inputs are finite; a program needn't handle non-finite values. No bound on the sum of `loss_mask` on one device may be relied on, other than what follows from the above.
Results may differ from a plain program's by a relative error of at most 0.0059.
Values may be sent and summed in bfloat16 or wider, within the bound.
A program may use at most 128 MiB of HBM per device.

v0:
```python
import jax
import jax.numpy as jnp
from jax import lax
from jax.sharding import PartitionSpec as P

D = 2048
BLOCK = 128
TLEN = 256


def gelu_tanh(value):
    return jax.nn.gelu(value, approximate=True)


def contributions(normed, tangent, wi_gate, wi_up, wo_weight):
    rows_dims = (((1,), (1,)), ((), ()))
    gate_pre = lax.dot_general(normed, wi_gate, rows_dims, preferred_element_type=jnp.float32)
    up_pre = lax.dot_general(normed, wi_up, rows_dims, preferred_element_type=jnp.float32)
    activated, pullback = jax.vjp(gelu_tanh, gate_pre)
    inner = (activated * up_pre).astype(jnp.bfloat16)
    back_grad = lax.dot_general(tangent, wo_weight, rows_dims, preferred_element_type=jnp.float32)
    grad_gate = pullback(back_grad * up_pre)[0].astype(jnp.bfloat16)
    grad_up = (back_grad * activated).astype(jnp.bfloat16)
    dims = (((0,), (0,)), ((), ()))
    first_grad = lax.dot_general(grad_gate, normed, dims, preferred_element_type=jnp.float32)
    second_grad = lax.dot_general(grad_up, normed, dims, preferred_element_type=jnp.float32)
    third_grad = lax.dot_general(inner, tangent, dims, preferred_element_type=jnp.float32)
    return jnp.stack([first_grad, second_grad, third_grad])


def on_device(hidden, gain, cotangent, blocks, loss_mask, wi_gate, wi_up, wo_weight):
    row_count = hidden.shape[2]
    micro_count = hidden.shape[1]
    position = lax.iota(jnp.int32, row_count)
    offset = position % TLEN
    sequence = position // TLEN
    picker = (sequence[None, :] == lax.iota(jnp.int32, blocks.shape[2])[:, None]).astype(jnp.int32)
    limit_pos = jnp.sum(blocks[0][:, :, None] * picker[None, :, :], axis=1) * BLOCK
    weight = (offset[None, :] < limit_pos).astype(jnp.int32) * loss_mask[0]
    token_total = lax.psum(jnp.sum(weight), "dp")
    denominator = jnp.maximum(token_total, 1).astype(jnp.float32)
    states = hidden[0].astype(jnp.float32)
    squares = lax.psum(jnp.sum(states * states, axis=-1), "mp")
    normed = (states * lax.rsqrt(squares / D + 1e-06)[:, :, None] * gain).astype(jnp.bfloat16)
    tangent = cotangent[0] * weight[:, :, None].astype(jnp.bfloat16)
    zeros_grad = jnp.zeros((3, wi_gate.shape[0], wi_gate.shape[1]), jnp.float32)
    running_sum = zeros_grad
    compensation = zeros_grad
    for micro_step in range(micro_count):
        whole_normed, whole_tangent = (
            lax.all_gather(normed[micro_step], "mp", axis=1, tiled=True),
            lax.all_gather(tangent[micro_step], "mp", axis=1, tiled=True),
        )
        contrib = contributions(whole_normed, whole_tangent, wi_gate, wi_up, wo_weight)
        adjusted = contrib - compensation
        running = running_sum + adjusted
        compensation = running - running_sum - adjusted
        running_sum = running
    share_part = lax.psum_scatter(running_sum, "dp", scatter_dimension=2, tiled=True)
    share_part = share_part / denominator
    result = lax.all_gather(share_part, "dp", axis=2, tiled=True)
    return result


def solution(mesh):
    return jax.shard_map(
        on_device,
        mesh=mesh,
        in_specs=(
            P("dp", None, None, "mp"),
            P("mp"),
            P("dp", None, None, "mp"),
            P("dp", None, None),
            P("dp", None, None),
            P("mp", None),
            P("mp", None),
            P("mp", None),
        ),
        out_specs=P(None, "mp", None),
        check_vma=False,
    )
```

profile of v0, /device:TPU:0, one launch (start us, length us, event | category | flops | bytes accessed | tf_op | source)
XLA Modules:
  0.0 716.0 jit_solution(7229344962575830412)
XLA Ops:
  8.3 23.4 %psum.14 = f32[4,512]{1,0:T(4,128)S(1)} all-reduce(f32[4,512]{1,0:T(4,128)S(1)} %fusion.1), channel_id=1, replica_groups=mesh['dp'=4,'mp'=8] {'mp'}, use_global_device_ids=true, to_apply=%region_2.3 | all-reduce | flops 2048 | bytes 16384 | tf_op jit(solution)/shard_map/psum | solution.py:43
  42.0 40.1 %all-gather.26.cloned.1.call-done = bf16[1,512,2048]{2,1,0:T(8,128)(2,1)} async-done(((bf16[1,512,256]{2,1,0:T(8,128)(2,1)}), bf16[1,512,2048]{2,1,0:T(8,128)(2,1)}) %all-gather.26.cloned.1.call-update) | async-done | bytes 2097168 | tf_op jit(solution)/shard_map/all_gather | solution.py:51
  82.1 4.5 fusion.24
  86.6 46.1 %all-gather.30.cloned.1.call-done = bf16[1,512,2048]{2,1,0:T(8,128)(2,1)} async-done(((bf16[1,512,256]{2,1,0:T(8,128)(2,1)}), bf16[1,512,2048]{2,1,0:T(8,128)(2,1)}) %all-gather.30.cloned.1.call-update) | async-done | bytes 2097168 | tf_op jit(solution)/shard_map/all_gather | solution.py:51
  132.7 4.6 fusion.15
  143.2 40.1 %all-gather.34.cloned.1.call-done = bf16[1,512,2048]{2,1,0:T(8,128)(2,1)} async-done(((bf16[1,512,256]{2,1,0:T(8,128)(2,1)}), bf16[1,512,2048]{2,1,0:T(8,128)(2,1)}) %all-gather.34.cloned.1.call-update) | async-done | bytes 2097168 | tf_op jit(solution)/shard_map/all_gather | solution.py:51
  183.3 4.6 fusion.6
  190.8 42.9 %all-gather.24.cloned.1.call-done = bf16[1,512,2048]{2,1,0:T(8,128)(2,1)} async-done(((bf16[1,512,256]{2,1,0:T(8,128)(2,1)}), bf16[1,512,2048]{2,1,0:T(8,128)(2,1)}) %all-gather.24.cloned.1.call-update) | async-done | bytes 2097168 | tf_op jit(solution)/shard_map/all_gather | solution.py:52
  233.8 5.3 fusion.29
  239.0 45.2 %all-gather.28.cloned.1.call-done = bf16[1,512,2048]{2,1,0:T(8,128)(2,1)} async-done(((bf16[1,512,256]{2,1,0:T(8,128)(2,1)}), bf16[1,512,2048]{2,1,0:T(8,128)(2,1)}) %all-gather.28.cloned.1.call-update) | async-done | bytes 2097168 | tf_op jit(solution)/shard_map/all_gather | solution.py:52
  284.2 4.4 fusion.20
  288.6 4.3 convolution_bitcast_fusion.6
  292.9 4.1 convolution_bitcast_fusion.7
  297.1 4.1 convolution_bitcast_fusion.3
  305.2 29.5 %all-gather.32.cloned.1.call-done = bf16[1,512,2048]{2,1,0:T(8,128)(2,1)} async-done(((bf16[1,512,256]{2,1,0:T(8,128)(2,1)}), bf16[1,512,2048]{2,1,0:T(8,128)(2,1)}) %all-gather.32.cloned.1.call-update) | async-done | bytes 2097168 | tf_op jit(solution)/shard_map/all_gather | solution.py:52
  334.7 6.6 convolution_bitcast_fusion
  344.2 4.1 convolution_bitcast_fusion.1
  348.2 37.0 %all-gather.22.cloned.1.call-done = bf16[1,512,2048]{2,1,0:T(8,128)(2,1)} async-done(((bf16[1,512,256]{2,1,0:T(8,128)(2,1)}), bf16[1,512,2048]{2,1,0:T(8,128)(2,1)}) %all-gather.22.cloned.1.call-update) | async-done | bytes 2097168 | tf_op jit(solution)/shard_map/all_gather | solution.py:51
  385.3 4.6 fusion.33
  393.1 4.6 convolution_bitcast_fusion.8
  397.8 4.7 convolution_bitcast_fusion.5
  402.5 4.6 convolution_bitcast_fusion.2
  407.0 28.8 %all-gather.20.cloned.1.call-done = bf16[1,512,2048]{2,1,0:T(8,128)(2,1)} async-done(((bf16[1,512,256]{2,1,0:T(8,128)(2,1)}), bf16[1,512,2048]{2,1,0:T(8,128)(2,1)}) %all-gather.20.cloned.1.call-update) | async-done | bytes 2097168 | tf_op jit(solution)/shard_map/all_gather | solution.py:52
  435.9 4.4 fusion.38
  440.3 4.4 convolution_bitcast_fusion.9
  444.7 5.2 convolution_bitcast_fusion.11
  454.0 20.6 %fusion = f32[3,640,2048]{2,1,0:T(8,128)} fusion(f32[1,640,2048]{2,1,0:T(8,128)} %convolution_bitcast_fusion, f32[1,640,2048]{2,1,0:T(8,128)} %convolution_bitcast_fusion.1, f32[1,640,2048]{2,1,0:T(8,128)} %convolution_bitcast_fusion.2, f32[1,640,2048]{2,1,0:T(8,128)S(1)} %bitcast.110, f32[1,640,2048]{2,1,0:T(8,128)S(1)} %bitcast.112, ...), kind=kLoop, calls=%fused_computation.4 | loop fusion | flops 74711040 | bytes 78643200 | tf_op jit(solution)/shard_map/add | solution.py:56
  474.7 5.5 psum.15
  480.9 108.6 %reduce-scatter.2.cloned.1.call-done = f32[3,640,512]{2,1,0:T(8,128)} async-done(((f32[3,640,2048]{2,1,0:T(8,128)}), f32[3,640,512]{2,1,0:T(8,128)}) %reduce-scatter.2.cloned.1.call-update) | async-done | bytes 3932176 | tf_op jit(solution)/shard_map/reduce_scatter | solution.py:59
  589.5 4.6 broadcast_divide_fusion
  594.2 100.1 %all-gather.18.cloned.1.call-done = f32[3,640,2048]{2,1,0:T(8,128)} async-done(((f32[3,640,512]{2,1,0:T(8,128)}), f32[3,640,2048]{2,1,0:T(8,128)}) %all-gather.18.cloned.1.call-update) | async-done | bytes 15728656 | tf_op jit(solution)/shard_map/all_gather | solution.py:61
  694.3 14.4 %copy.11 = f32[3,640,2048]{2,1,0:T(8,128)} copy(f32[3,640,2048]{2,1,0:T(8,128)} %all-gather.18.cloned.1.call-done) | data formatting | bytes 31457280
  (142 shorter events, 34.9 us)
Async XLA Ops:
  6.5 75.5 %copy-start = (bf16[640,2048]{1,0:T(8,128)(2,1)S(1)}, bf16[640,2048]{1,0:T(8,128)(2,1)}, u32[]{:S(2)}) copy-start(bf16[640,2048]{1,0:T(8,128)(2,1)} %param.13) | copy-start | bytes 7864324
  6.5 75.5 %all-gather.26.cloned.1.call-start = ((), (), s32[]{:S(2)}) async-start(), calls=%async_computation.6 | async-start | bytes 2359296 | tf_op jit(solution)/shard_map/all_gather | solution.py:51
  34.3 98.4 %all-gather.30.cloned.1.call-start = ((), (), s32[]{:S(2)}) async-start(), calls=%async_computation.8 | async-start | bytes 2359296 | tf_op jit(solution)/shard_map/all_gather | solution.py:51
  35.1 148.2 %all-gather.34.cloned.1.call-start = ((), (), s32[]{:S(2)}) async-start(), calls=%async_computation.10 | async-start | bytes 2359296 | tf_op jit(solution)/shard_map/all_gather | solution.py:51
  35.8 197.9 %all-gather.24.cloned.1.call-start = ((), (), s32[]{:S(2)}) async-start(), calls=%async_computation.5 | async-start | bytes 2359296 | tf_op jit(solution)/shard_map/all_gather | solution.py:52
  39.3 244.9 %all-gather.28.cloned.1.call-start = ((), (), s32[]{:S(2)}) async-start(), calls=%async_computation.7 | async-start | bytes 2359296 | tf_op jit(solution)/shard_map/all_gather | solution.py:52
  39.8 294.8 %all-gather.32.cloned.1.call-start = ((), (), s32[]{:S(2)}) async-start(), calls=%async_computation.9 | async-start | bytes 2359296 | tf_op jit(solution)/shard_map/all_gather | solution.py:52
  40.4 344.8 %all-gather.22.cloned.1.call-start = ((), (), s32[]{:S(2)}) async-start(), calls=%async_computation.4 | async-start | bytes 2359296 | tf_op jit(solution)/shard_map/all_gather | solution.py:51
  41.2 394.7 %all-gather.20.cloned.1.call-start = ((), (), s32[]{:S(2)}) async-start(), calls=%async_computation.3 | async-start | bytes 2359296 | tf_op jit(solution)/shard_map/all_gather | solution.py:52
  41.9 547.6 %reduce-scatter.2.cloned.1.call-start = ((), (), s32[]{:S(2)}) async-start(), calls=%async_computation.1 | async-start | bytes 19660800 | tf_op jit(solution)/shard_map/reduce_scatter | solution.py:59
  288.6 12.6 %copy-start.31 = (f32[512,640]{1,0:T(8,128)}, f32[512,640]{1,0:T(8,128)S(1)}, u32[]{:S(2)}) copy-start(f32[512,640]{1,0:T(8,128)S(1)} %fusion.20) | copy-start | bytes 3932164
  334.7 6.6 copy-start.23
  334.7 6.6 copy-start.41
  393.1 4.7 copy-start.5
  393.1 4.7 copy-start.14
  397.7 4.7 copy-start.7
  397.7 4.7 copy-start.17
  397.8 4.7 copy-start.26
  397.8 4.7 copy-start.35
  407.0 33.2 %copy-start.8 = (f32[512,640]{1,0:T(8,128)S(1)}, f32[512,640]{1,0:T(8,128)}, u32[]{:S(2)}) copy-start(f32[512,640]{1,0:T(8,128)} %fusion.33) | copy-start | bytes 3932164
  407.0 33.2 %copy-start.33 = (f32[512,640]{1,0:T(8,128)S(1)}, f32[512,640]{1,0:T(8,128)}, u32[]{:S(2)}) copy-start(f32[512,640]{1,0:T(8,128)} %fusion.35) | copy-start | bytes 3932164
  435.9 8.8 %copy-start.19 = (bf16[1,512,2048]{2,1,0:T(8,128)(2,1)S(1)}, bf16[1,512,2048]{2,1,0:T(8,128)(2,1)}, u32[]{:S(2)}) copy-start(bf16[1,512,2048]{2,1,0:T(8,128)(2,1)} %all-gather.22.cloned.1.call-done) | copy-start | bytes 6291460
  440.3 13.7 %slice-start = ((s8[5242880]{0:T(1024)(128)(4,1)}), s8[4194304]{0:T(1024)(128)(4,1)S(1)}, s32[]{:S(2)}) async-start(s8[5242880]{0:T(1024)(128)(4,1)} %bitcast.105), calls=%async_computation.11 | async-start | bytes 8388608
  440.3 13.7 %slice-start.2 = ((s8[5242880]{0:T(1024)(128)(4,1)}), s8[4194304]{0:T(1024)(128)(4,1)S(1)}, s32[]{:S(2)}) async-start(s8[5242880]{0:T(1024)(128)(4,1)} %bitcast.107), calls=%async_computation.13 | async-start | bytes 8388608
  440.3 13.7 %slice-start.4 = ((s8[5242880]{0:T(1024)(128)(4,1)}), s8[4194304]{0:T(1024)(128)(4,1)S(1)}, s32[]{:S(2)}) async-start(s8[5242880]{0:T(1024)(128)(4,1)} %bitcast.109), calls=%async_computation.15 | async-start | bytes 8388608
  440.3 13.7 %slice-start.6 = ((s8[5242880]{0:T(1024)(128)(4,1)}), s8[4194304]{0:T(1024)(128)(4,1)S(1)}, s32[]{:S(2)}) async-start(s8[5242880]{0:T(1024)(128)(4,1)} %bitcast.111), calls=%async_computation.17 | async-start | bytes 8388608
  444.7 9.2 %slice-start.1 = ((s8[5242880]{0:T(1024)(128)(4,1)}), s8[1048576]{0:T(1024)(128)(4,1)S(1)}, s32[]{:S(2)}) async-start(s8[5242880]{0:T(1024)(128)(4,1)} %bitcast.105), calls=%async_computation.12 | async-start | bytes 2097152
  444.7 9.3 %slice-start.3 = ((s8[5242880]{0:T(1024)(128)(4,1)}), s8[1048576]{0:T(1024)(128)(4,1)S(1)}, s32[]{:S(2)}) async-start(s8[5242880]{0:T(1024)(128)(4,1)} %bitcast.107), calls=%async_computation.14 | async-start | bytes 2097152
  444.7 9.3 %slice-start.5 = ((s8[5242880]{0:T(1024)(128)(4,1)}), s8[1048576]{0:T(1024)(128)(4,1)S(1)}, s32[]{:S(2)}) async-start(s8[5242880]{0:T(1024)(128)(4,1)} %bitcast.109), calls=%async_computation.16 | async-start | bytes 2097152
  444.7 9.3 %slice-start.7 = ((s8[5242880]{0:T(1024)(128)(4,1)}), s8[1048576]{0:T(1024)(128)(4,1)S(1)}, s32[]{:S(2)}) async-start(s8[5242880]{0:T(1024)(128)(4,1)} %bitcast.111), calls=%async_computation.18 | async-start | bytes 2097152
  474.7 219.7 %all-gather.18.cloned.1.call-start = ((), (), s32[]{:S(2)}) async-start(), calls=%async_computation.2 | async-start | bytes 19660800 | tf_op jit(solution)/shard_map/all_gather | solution.py:61
  694.3 14.4 %copy-start.1 = (bf16[640,2048]{1,0:T(8,128)(2,1)S(1)}, bf16[640,2048]{1,0:T(8,128)(2,1)}, u32[]{:S(2)}) copy-start(bf16[640,2048]{1,0:T(8,128)(2,1)} %param.13) | copy-start | bytes 7864324
  (28 other events, 107.5 us)
Sparse Core Ops, SparseCore 0:
  34.4 47.5 all-gather.25
  84.1 48.5 all-gather.29
  134.7 48.5 all-gather.33
  185.2 48.5 all-gather.23
  235.6 48.5 all-gather.27
  286.1 48.5 all-gather.31
  336.7 48.5 all-gather.21
  387.3 48.5 all-gather.19
  474.8 114.7 reduce-scatter.1
  594.3 99.9 all-gather.17
where the time goes:
time: 726 us; the launch traced here: 716 us
  waiting for transfers between devices  522 us (72%)
  matrix products  101 us (14%)
  other arithmetic  30.9 us (4%)
  blocking collectives  28.9 us (4%)
  local copies, waits for them, and re-layouts  17.7 us (2%)
  between operations  15.1 us (2%)
    all_gather x4, waiting for transfers between devices, on_device(): lax.all_gather(normed[micro_step], 'mp', axis=1, tiled=True)  163 us
    all_gather x4, waiting for transfers between devices, on_device(): lax.all_gather(tangent[micro_step], 'mp', axis=1, tiled=True)  146 us
    reduce_scatter x1, waiting for transfers between devices, on_device(): lax.psum_scatter(running_sum, 'dp', scatter_dimension=2, tiled=True)  109 us
    all_gather x1, waiting for transfers between devices, on_device(): result = lax.all_gather(share_part, 'dp', axis=2, tiled=True)  100 us
    psum x1, blocking collectives, on_device(): squares = lax.psum(jnp.sum(states * states, axis=-1), 'mp')  23.4 us
    add x1, other arithmetic, on_device(): running = running_sum + adjusted  20.6 us
    dot_general x4, matrix products, contributions(): lax.dot_general(inner, tangent, dims, preferred_element_type=jnp.float32)  19.3 us
    dot_general x4, matrix products, contributions(): lax.dot_general(grad_gate, normed, dims, preferred_element_type=jnp.float32)  19.1 us
  transfers between devices with their start and end apart: 10, of which 10 were waited for; matrix products, arithmetic and copies ran while one was open for 12% of the time, Pallas kernels for 0%

commit v1 on v0

--- a/solution.py
+++ b/solution.py
@@ -58,7 +58,12 @@
         running_sum = running
     share_part = lax.psum_scatter(running_sum, "dp", scatter_dimension=2, tiled=True)
     share_part = share_part / denominator
-    result = lax.all_gather(share_part, "dp", axis=2, tiled=True)
+    ring = [share_part]
+    for hop in range(3):
+        ring.append(lax.ppermute(ring[-1], "dp", [(dev, (dev + 1) % 4) for dev in range(4)]))
+    result = jnp.roll(
+        jnp.concatenate(ring[::-1], axis=2), (lax.axis_index("dp") + 1) * ring[0].shape[2], axis=2
+    )
     return result
 
 

time: 726 us -> 790 us (1.088)
  waiting for transfers between devices: 522 us -> 558 us
  local copies, waits for them, and re-layouts: 17.7 us -> 43.2 us
    ppermute x0 -> x3, waiting for transfers between devices: none -> 136 us  [on_device(): lax.ppermute(ring[-1], 'dp', [(dev, (dev + 1) % 4) for dev in range(4)])]
    all_gather x1 -> x0, waiting for transfers between devices: 100 us -> none  [on_device(): result = lax.all_gather(share_part, 'dp', axis=2, tiled=True)]
    all_gather x4, waiting for transfers between devices: 146 us -> 165 us  [on_device(): lax.all_gather(tangent[micro_step], 'mp', axis=1, tiled=True)]
    all_gather x4, waiting for transfers between devices: 163 us -> 145 us  [on_device(): lax.all_gather(normed[micro_step], 'mp', axis=1, tiled=True)]
    dynamic_slice x0 -> x1, local copies, waits for them, and re-layouts: none -> 14.4 us  [on_device(): jnp.roll(jnp.concatenate(ring[::-1], axis=2), (lax.axis_index('dp') + 1)...]
    unnamed x101 -> x112, local copies, waits for them, and re-layouts: 15.7 us -> 26.8 us
  transfers between devices with their start and end apart: 10 -> 12, of which waited for: 10 -> 12; matrix products, arithmetic and copies ran while one was open for 12% -> 11% of each run, Pallas kernels for 0% -> 0%
where the time goes in v1:
time: 790 us; the launch traced here: 780 us
  waiting for transfers between devices  558 us (71%)
  matrix products  101 us (13%)
  local copies, waits for them, and re-layouts  43.2 us (5%)
  other arithmetic  33.6 us (4%)
  blocking collectives  28.9 us (4%)
  between operations  14.8 us (2%)
    all_gather x4, waiting for transfers between devices, on_device(): lax.all_gather(tangent[micro_step], 'mp', axis=1, tiled=True)  165 us
    all_gather x4, waiting for transfers between devices, on_device(): lax.all_gather(normed[micro_step], 'mp', axis=1, tiled=True)  145 us
    ppermute x3, waiting for transfers between devices, on_device(): lax.ppermute(ring[-1], 'dp', [(dev, (dev + 1) % 4) for dev in range(4)])  136 us
    reduce_scatter x1, waiting for transfers between devices, on_device(): lax.psum_scatter(running_sum, 'dp', scatter_dimension=2, tiled=True)  109 us
    unnamed x112, local copies, waits for them, and re-layouts  26.8 us
    psum x1, blocking collectives, on_device(): squares = lax.psum(jnp.sum(states * states, axis=-1), 'mp')  23.4 us
    add x1, other arithmetic, on_device(): running = running_sum + adjusted  20.6 us
    dot_general x4, matrix products, contributions(): lax.dot_general(tangent, wo_weight, rows_dims, preferred_element_type=jnp...  19.3 us
  transfers between devices with their start and end apart: 12, of which 12 were waited for; matrix products, arithmetic and copies ran while one was open for 11% of the time, Pallas kernels for 0%

profile of v1, /device:TPU:0, one launch (start us, length us, event | category | flops | bytes accessed | tf_op | source)
XLA Modules:
  0.0 779.6 jit_solution(18427025968081392425)
XLA Ops:
  8.3 23.4 %psum.14 = f32[4,512]{1,0:T(4,128)S(1)} all-reduce(f32[4,512]{1,0:T(4,128)S(1)} %fusion.1), channel_id=1, replica_groups=mesh['dp'=4,'mp'=8] {'mp'}, use_global_device_ids=true, to_apply=%region_2.3 | all-reduce | flops 2048 | bytes 16384 | tf_op jit(solution)/shard_map/psum | solution.py:43
  42.0 40.1 %all-gather.27.cloned.1.call-done = bf16[1,512,2048]{2,1,0:T(8,128)(2,1)} async-done(((bf16[1,512,256]{2,1,0:T(8,128)(2,1)}), bf16[1,512,2048]{2,1,0:T(8,128)(2,1)}) %all-gather.27.cloned.1.call-update) | async-done | bytes 2097168 | tf_op jit(solution)/shard_map/all_gather | solution.py:51
  82.1 4.6 fusion.15
  89.7 43.0 %all-gather.23.cloned.1.call-done = bf16[1,512,2048]{2,1,0:T(8,128)(2,1)} async-done(((bf16[1,512,256]{2,1,0:T(8,128)(2,1)}), bf16[1,512,2048]{2,1,0:T(8,128)(2,1)}) %all-gather.23.cloned.1.call-update) | async-done | bytes 2097168 | tf_op jit(solution)/shard_map/all_gather | solution.py:51
  132.7 4.6 fusion.24
  140.2 43.1 %all-gather.19.cloned.1.call-done = bf16[1,512,2048]{2,1,0:T(8,128)(2,1)} async-done(((bf16[1,512,256]{2,1,0:T(8,128)(2,1)}), bf16[1,512,2048]{2,1,0:T(8,128)(2,1)}) %all-gather.19.cloned.1.call-update) | async-done | bytes 2097168 | tf_op jit(solution)/shard_map/all_gather | solution.py:51
  183.3 4.5 fusion.33
  187.8 46.0 %all-gather.17.cloned.1.call-done = bf16[1,512,2048]{2,1,0:T(8,128)(2,1)} async-done(((bf16[1,512,256]{2,1,0:T(8,128)(2,1)}), bf16[1,512,2048]{2,1,0:T(8,128)(2,1)}) %all-gather.17.cloned.1.call-update) | async-done | bytes 2097168 | tf_op jit(solution)/shard_map/all_gather | solution.py:52
  233.8 5.3 fusion.38
  239.1 45.1 %all-gather.25.cloned.1.call-done = bf16[1,512,2048]{2,1,0:T(8,128)(2,1)} async-done(((bf16[1,512,256]{2,1,0:T(8,128)(2,1)}), bf16[1,512,2048]{2,1,0:T(8,128)(2,1)}) %all-gather.25.cloned.1.call-update) | async-done | bytes 2097168 | tf_op jit(solution)/shard_map/all_gather | solution.py:52
  284.2 5.2 fusion.20
  289.5 45.2 %all-gather.21.cloned.1.call-done = bf16[1,512,2048]{2,1,0:T(8,128)(2,1)} async-done(((bf16[1,512,256]{2,1,0:T(8,128)(2,1)}), bf16[1,512,2048]{2,1,0:T(8,128)(2,1)}) %all-gather.21.cloned.1.call-update) | async-done | bytes 2097168 | tf_op jit(solution)/shard_map/all_gather | solution.py:52
  334.7 4.4 fusion.29
  366.7 18.6 %all-gather.31.cloned.1.call-done = bf16[1,512,2048]{2,1,0:T(8,128)(2,1)} async-done(((bf16[1,512,256]{2,1,0:T(8,128)(2,1)}), bf16[1,512,2048]{2,1,0:T(8,128)(2,1)}) %all-gather.31.cloned.1.call-update) | async-done | bytes 2097168 | tf_op jit(solution)/shard_map/all_gather | solution.py:51
  385.3 4.7 fusion.6
  393.2 4.6 convolution_bitcast_fusion.11
  397.9 4.7 convolution_bitcast_fusion.5
  402.6 4.6 convolution_bitcast_fusion.8
  407.1 28.8 %all-gather.29.cloned.1.call-done = bf16[1,512,2048]{2,1,0:T(8,128)(2,1)} async-done(((bf16[1,512,256]{2,1,0:T(8,128)(2,1)}), bf16[1,512,2048]{2,1,0:T(8,128)(2,1)}) %all-gather.29.cloned.1.call-update) | async-done | bytes 2097168 | tf_op jit(solution)/shard_map/all_gather | solution.py:52
  440.3 4.4 convolution_bitcast_fusion.1
  444.8 5.2 convolution_bitcast_fusion.2
  454.1 20.6 %fusion = f32[3,640,2048]{2,1,0:T(8,128)} fusion(f32[1,640,2048]{2,1,0:T(8,128)} %convolution_bitcast_fusion, f32[1,640,2048]{2,1,0:T(8,128)} %convolution_bitcast_fusion.1, f32[1,640,2048]{2,1,0:T(8,128)} %convolution_bitcast_fusion.2, f32[1,640,2048]{2,1,0:T(8,128)S(1)} %bitcast.106, f32[1,640,2048]{2,1,0:T(8,128)S(1)} %bitcast.108, ...), kind=kLoop, calls=%fused_computation.4 | loop fusion | flops 74711040 | bytes 78643200 | tf_op jit(solution)/shard_map/add | solution.py:56
  474.7 5.5 psum.15
  480.9 108.7 %reduce-scatter.2.cloned.1.call-done = f32[3,640,512]{2,1,0:T(8,128)} async-done(((f32[3,640,2048]{2,1,0:T(8,128)}), f32[3,640,512]{2,1,0:T(8,128)}) %reduce-scatter.2.cloned.1.call-update) | async-done | bytes 3932176 | tf_op jit(solution)/shard_map/reduce_scatter | solution.py:59
  592.2 45.1 %collective-permute-done = f32[3,640,512]{2,1,0:T(8,128)S(1)} collective-permute-done((f32[3,640,512]{2,1,0:T(8,128)S(1)}, f32[3,640,512]{2,1,0:T(8,128)S(1)}, u32[]{:S(2)}, u32[]{:S(2)}) %collective-permute-start) | collective-permute-done | bytes 3932192 | tf_op jit(solution)/shard_map/ppermute | solution.py:63
  639.3 45.2 %collective-permute-done.1 = f32[3,640,512]{2,1,0:T(8,128)} collective-permute-done((f32[3,640,512]{2,1,0:T(8,128)S(1)}, f32[3,640,512]{2,1,0:T(8,128)}, u32[]{:S(2)}, u32[]{:S(2)}) %collective-permute-start.1) | collective-permute-done | bytes 3932192 | tf_op jit(solution)/shard_map/ppermute | solution.py:63
  684.5 45.4 %collective-permute-done.2 = f32[3,640,512]{2,1,0:T(8,128)} collective-permute-done((f32[3,640,512]{2,1,0:T(8,128)}, f32[3,640,512]{2,1,0:T(8,128)}, u32[]{:S(2)}, u32[]{:S(2)}) %collective-permute-start.2) | collective-permute-done | bytes 3932192 | tf_op jit(solution)/shard_map/ppermute | solution.py:63
  729.9 4.4 constant_dynamic-update-slice_fusion.7
  734.3 4.6 constant_dynamic-update-slice_fusion.6
  744.8 4.5 constant_dynamic-update-slice_fusion.3
  749.2 4.4 constant_dynamic-update-slice_fusion.2
  758.2 14.4 %constant_dynamic-slice_fusion = f32[3,640,2048]{2,1,0:T(8,128)} fusion(f32[3,640,4096]{2,1,0:T(8,128)} %constant_dynamic-update-slice_fusion, s32[]{:T(128)S(6)} %select_n.35), kind=kLoop, calls=%fused_computation.155 | loop fusion | bytes 31457284 | tf_op jit(solution)/shard_map/jit(_roll_dynamic)/dynamic_slice | solution.py:64
  (159 shorter events, 72.0 us)
Async XLA Ops:
  6.5 75.6 %copy-start = (bf16[640,2048]{1,0:T(8,128)(2,1)S(1)}, bf16[640,2048]{1,0:T(8,128)(2,1)}, u32[]{:S(2)}) copy-start(bf16[640,2048]{1,0:T(8,128)(2,1)} %param.13) | copy-start | bytes 7864324
  6.5 75.6 %all-gather.27.cloned.1.call-start = ((), (), s32[]{:S(2)}) async-start(), calls=%async_computation.7 | async-start | bytes 2359296 | tf_op jit(solution)/shard_map/all_gather | solution.py:51
  34.3 98.4 %all-gather.23.cloned.1.call-start = ((), (), s32[]{:S(2)}) async-start(), calls=%async_computation.5 | async-start | bytes 2359296 | tf_op jit(solution)/shard_map/all_gather | solution.py:51
  35.1 148.2 %all-gather.19.cloned.1.call-start = ((), (), s32[]{:S(2)}) async-start(), calls=%async_computation.3 | async-start | bytes 2359296 | tf_op jit(solution)/shard_map/all_gather | solution.py:51
  35.8 197.9 %all-gather.17.cloned.1.call-start = ((), (), s32[]{:S(2)}) async-start(), calls=%async_computation.2 | async-start | bytes 2359296 | tf_op jit(solution)/shard_map/all_gather | solution.py:52
  39.3 244.9 %all-gather.25.cloned.1.call-start = ((), (), s32[]{:S(2)}) async-start(), calls=%async_computation.6 | async-start | bytes 2359296 | tf_op jit(solution)/shard_map/all_gather | solution.py:52
  39.9 294.8 %all-gather.21.cloned.1.call-start = ((), (), s32[]{:S(2)}) async-start(), calls=%async_computation.4 | async-start | bytes 2359296 | tf_op jit(solution)/shard_map/all_gather | solution.py:52
  40.5 344.8 %all-gather.31.cloned.1.call-start = ((), (), s32[]{:S(2)}) async-start(), calls=%async_computation.9 | async-start | bytes 2359296 | tf_op jit(solution)/shard_map/all_gather | solution.py:51
  41.2 394.7 %all-gather.29.cloned.1.call-start = ((), (), s32[]{:S(2)}) async-start(), calls=%async_computation.8 | async-start | bytes 2359296 | tf_op jit(solution)/shard_map/all_gather | solution.py:52
  42.0 547.6 %reduce-scatter.2.cloned.1.call-start = ((), (), s32[]{:S(2)}) async-start(), calls=%async_computation.1 | async-start | bytes 19660800 | tf_op jit(solution)/shard_map/reduce_scatter | solution.py:59
  339.1 12.5 %copy-start.32 = (f32[512,640]{1,0:T(8,128)}, f32[512,640]{1,0:T(8,128)S(1)}, u32[]{:S(2)}) copy-start(f32[512,640]{1,0:T(8,128)S(1)} %fusion.29) | copy-start | bytes 3932164
  385.3 4.7 copy-start.21
  385.3 4.7 copy-start.44
  397.8 4.7 copy-start.8
  397.8 4.7 copy-start.17
  397.9 4.7 copy-start.29
  397.9 4.7 copy-start.33
  407.1 33.1 %copy-start.11 = (f32[512,640]{1,0:T(8,128)S(1)}, f32[512,640]{1,0:T(8,128)}, u32[]{:S(2)}) copy-start(f32[512,640]{1,0:T(8,128)} %fusion.6) | copy-start | bytes 3932164
  435.9 8.8 %copy-start.36 = (f32[512,640]{1,0:T(8,128)S(1)}, f32[512,640]{1,0:T(8,128)}, u32[]{:S(2)}) copy-start(f32[512,640]{1,0:T(8,128)} %fusion.8) | copy-start | bytes 3932164
  440.3 13.7 %slice-start = ((s8[5242880]{0:T(1024)(128)(4,1)}), s8[4194304]{0:T(1024)(128)(4,1)S(1)}, s32[]{:S(2)}) async-start(s8[5242880]{0:T(1024)(128)(4,1)} %bitcast.105), calls=%async_computation.10 | async-start | bytes 8388608
  440.3 13.7 %slice-start.2 = ((s8[5242880]{0:T(1024)(128)(4,1)}), s8[4194304]{0:T(1024)(128)(4,1)S(1)}, s32[]{:S(2)}) async-start(s8[5242880]{0:T(1024)(128)(4,1)} %bitcast.107), calls=%async_computation.12 | async-start | bytes 8388608
  440.3 13.7 %slice-start.4 = ((s8[5242880]{0:T(1024)(128)(4,1)}), s8[4194304]{0:T(1024)(128)(4,1)S(1)}, s32[]{:S(2)}) async-start(s8[5242880]{0:T(1024)(128)(4,1)} %bitcast.109), calls=%async_computation.14 | async-start | bytes 8388608
  440.3 13.7 %slice-start.6 = ((s8[5242880]{0:T(1024)(128)(4,1)}), s8[4194304]{0:T(1024)(128)(4,1)S(1)}, s32[]{:S(2)}) async-start(s8[5242880]{0:T(1024)(128)(4,1)} %bitcast.111), calls=%async_computation.16 | async-start | bytes 8388608
  444.7 5.2 copy-start.23
  444.7 9.3 %slice-start.1 = ((s8[5242880]{0:T(1024)(128)(4,1)}), s8[1048576]{0:T(1024)(128)(4,1)S(1)}, s32[]{:S(2)}) async-start(s8[5242880]{0:T(1024)(128)(4,1)} %bitcast.105), calls=%async_computation.11 | async-start | bytes 2097152
  444.7 9.3 %slice-start.3 = ((s8[5242880]{0:T(1024)(128)(4,1)}), s8[1048576]{0:T(1024)(128)(4,1)S(1)}, s32[]{:S(2)}) async-start(s8[5242880]{0:T(1024)(128)(4,1)} %bitcast.107), calls=%async_computation.13 | async-start | bytes 2097152
  444.7 9.3 %slice-start.5 = ((s8[5242880]{0:T(1024)(128)(4,1)}), s8[1048576]{0:T(1024)(128)(4,1)S(1)}, s32[]{:S(2)}) async-start(s8[5242880]{0:T(1024)(128)(4,1)} %bitcast.109), calls=%async_computation.15 | async-start | bytes 2097152
  444.8 9.3 %slice-start.7 = ((s8[5242880]{0:T(1024)(128)(4,1)}), s8[1048576]{0:T(1024)(128)(4,1)S(1)}, s32[]{:S(2)}) async-start(s8[5242880]{0:T(1024)(128)(4,1)} %bitcast.111), calls=%async_computation.17 | async-start | bytes 2097152
  592.2 45.2 %collective-permute-start = (f32[3,640,512]{2,1,0:T(8,128)S(1)}, f32[3,640,512]{2,1,0:T(8,128)S(1)}, u32[]{:S(2)}, u32[]{:S(2)}) collective-permute-start(f32[3,640,512]{2,1,0:T(8,128)S(1)} %broadcast_divide_fusion), channel_id=1, source_target_pairs={{0,8},{8,16},{16,24},{24,0},{1,9},{9,17},{17,25},{25,1},{2,10},{10... | collective-permute-start | bytes 11796488 | tf_op jit(solution)/shard_map/ppermute | solution.py:63
  639.3 45.2 %collective-permute-start.1 = (f32[3,640,512]{2,1,0:T(8,128)S(1)}, f32[3,640,512]{2,1,0:T(8,128)}, u32[]{:S(2)}, u32[]{:S(2)}) collective-permute-start(f32[3,640,512]{2,1,0:T(8,128)S(1)} %collective-permute-done), channel_id=1, source_target_pairs={{0,8},{8,16},{16,24},{24,0},{1,9},{9,17},{17,25},{25,1},{2,10},{10... | collective-permute-start | bytes 11796488 | tf_op jit(solution)/shard_map/ppermute | solution.py:63
  684.5 45.4 %collective-permute-start.2 = (f32[3,640,512]{2,1,0:T(8,128)}, f32[3,640,512]{2,1,0:T(8,128)}, u32[]{:S(2)}, u32[]{:S(2)}) collective-permute-start(f32[3,640,512]{2,1,0:T(8,128)} %collective-permute-done.1), channel_id=1, source_target_pairs={{0,8},{8,16},{16,24},{24,0},{1,9},{9,17},{17,25},{25,1},{2,10},{10... | collective-permute-start | bytes 11796488 | tf_op jit(solution)/shard_map/ppermute | solution.py:63
  758.2 14.4 %copy-start.1 = (bf16[640,2048]{1,0:T(8,128)(2,1)S(1)}, bf16[640,2048]{1,0:T(8,128)(2,1)}, u32[]{:S(2)}) copy-start(bf16[640,2048]{1,0:T(8,128)(2,1)} %param.13) | copy-start | bytes 7864324
  (33 other events, 127.9 us)
Sparse Core Ops, SparseCore 0:
  34.5 47.5 all-gather.26
  84.1 48.5 all-gather.22
  134.7 48.5 all-gather.18
  185.2 48.5 all-gather.16
  235.7 48.5 all-gather.24
  286.1 48.5 all-gather.20
  336.7 48.5 all-gather.30
  387.3 48.5 all-gather.28
  474.8 114.7 reduce-scatter.1
